TPU v7x, 32 devices: a whole 2x2x4 slice. The times are simulated.
32 devices in a mesh: grp: 4 (over z), sep: 8 (over y, x, core).
Axes of the slice: x: 2, y: 2, z: 4, core: 2. Of those that a mesh axis runs over, the one named last changes fastest.
Arguments:
- tiles: bfloat16 [4, 256, 64, 128], P('grp', 'sep'), may hold values from 0.0099487305 to 0.29882812
- tile_front: int32 [4, 256, 1], P('grp', 'sep'), may hold values from 0 to 7; in each aligned block of 32 rows (0 to 31, 32 to 63, ..., all dimensions but the last counted through in order) at most 8 rows name the same one
- tile_pos: int32 [4, 256], P('grp', 'sep'), may hold values from 0 to 29
- front_slot: int32 [4, 8], P('grp'), may hold values from 0 to 7, as said below
- front_parent: int32 [4, 8], P('grp'), may hold values from 0 to 7, as said below
- pivot: float32 [4, 8, 640], P('grp'), may hold values from 4 to 40
Outputs:
- factor: float32 [4, 8, 640, 512], P('grp', 'sep')
- sep_schur: float32 [8, 128, 128], P('sep')
Inputs may be any that keep to these rules, and one draw needn't show every extreme that they name: `tile_front`: at most 8 of the tiles held by one device belong to one front. `front_slot`: each group's row is a permutation of 0 to 7. (front_parent[g, f] - front_slot[g, f]) modulo 8 is one of 0, 1, 7 and 4; in every group each of these four occurs.
All inputs are finite; a program needn't handle non-finite values.
Results may differ from a plain program's by a relative error of at most 0.0003.
Values may be sent and summed in bfloat16 or wider, within the bound.
A program may use at most 64 MiB of HBM per device.

v0:
```python
import jax
import jax.numpy as jnp
import numpy as np
from jax import lax
from jax.sharding import PartitionSpec as P

POS = 30


def passed_along(shard, axis, by):
    devices = lax.axis_size(axis)
    return lax.ppermute(shard, axis, [(i, (i + by) % devices) for i in range(devices)])


def tile_arrangement(rows, column_indices):
    row_count = 5 * column_indices // rows
    position = np.zeros((row_count, 5), np.int32)
    present = np.zeros((row_count, 5), np.float32)
    number = 0
    for row_block in range(row_count):
        for col_block in range(row_block * rows // column_indices + 1):
            position[row_block, col_block] = number
            present[row_block, col_block] = 1.0
            number += 1
    return (position, present)


def front_factor(summed, pivots, rows, column_indices):
    position, present = tile_arrangement(rows, column_indices)
    order = 5 * column_indices
    elimination_count = 4 * column_indices
    blocks = summed[position] * jnp.asarray(present, jnp.float32)[:, :, None, None]
    full = blocks.transpose(0, 2, 1, 3).reshape(order, order)
    mixed = 0.5 * (full + full.T) * (1.0 - jnp.eye(order, dtype=jnp.float32))
    front_matrix = jnp.diag(pivots + jnp.sum(mixed, 1)) - mixed
    lower_triangle = jnp.linalg.cholesky(front_matrix[:elimination_count, :elimination_count])
    under_diagonal = jax.scipy.linalg.solve_triangular(
        lower_triangle, front_matrix[elimination_count:, :elimination_count].T, lower=True
    ).T
    schur = jnp.dot(under_diagonal, under_diagonal.T, precision=lax.Precision.HIGHEST)
    return (jnp.concatenate([lower_triangle, under_diagonal], 0), schur)


def body(tiles, tile_front, tile_pos, front_slot, front_parent, pivot):
    width = lax.axis_size("sep")
    myself = lax.axis_index("sep")
    held = tiles.shape[1]
    rows = tiles.shape[2]
    column_indices = tiles.shape[3]
    fronts = front_slot.shape[1]
    room = max(2, -(-2 * held // width))
    slots = front_slot[0]
    parents = front_parent[0]
    front_ids = jnp.arange(fronts, dtype=jnp.int32)
    owner_of = jnp.sum(jnp.where(tile_front[0] == front_ids[None, :], slots[None, :], 0), 1)
    target = (owner_of[:, None] == jnp.arange(width, dtype=jnp.int32)[None, :]).astype(jnp.int32)
    rank = jnp.sum(target * (jnp.cumsum(target, 0) - 1), 1)
    place = owner_of * room + rank
    outgoing = jnp.zeros((width * room, rows, column_indices), jnp.bfloat16).at[place].set(tiles[0])
    labels = jnp.full((width * room,), -1, jnp.int32).at[place].set(tile_pos[0])
    arrived, received_position = (
        lax.all_to_all(
            outgoing.reshape(width, room, rows, column_indices),
            "sep",
            split_axis=0,
            concat_axis=0,
            tiled=True,
        ),
        lax.all_to_all(labels.reshape(width, room), "sep", split_axis=0, concat_axis=0, tiled=True),
    )
    arrived = arrived.reshape(width * room, rows, column_indices)
    received_position = received_position.reshape(width * room)
    selector = (received_position[None, :] == jnp.arange(POS, dtype=jnp.int32)[:, None]).astype(
        jnp.bfloat16
    )
    summed = jnp.einsum("ps,sij->pij", selector, arrived, preferred_element_type=jnp.float32)
    mine = slots == myself
    pivots = jnp.sum(jnp.where(mine[:, None], pivot[0], 0.0), 0)
    parent = jnp.sum(jnp.where(mine, parents, 0))
    factor, schur = front_factor(summed, pivots, rows, column_indices)
    distance = (parent - myself) % width
    local_sum = jnp.where(distance == 0, schur, 0.0)[None]
    for offset in (1, -1, width // 2):
        piece = jnp.where(distance == offset % width, schur, 0.0)[None]
        local_sum = local_sum + passed_along(piece, "sep", offset)
    total = lax.psum(local_sum, "grp")
    return (factor[None, None], total)


def solution(mesh):
    placed = (
        P("grp", "sep", None, None),
        P("grp", "sep", None),
        P("grp", "sep"),
        P("grp", None),
        P("grp", None),
        P("grp", None, None),
    )
    return jax.shard_map(
        body,
        mesh=mesh,
        in_specs=placed,
        out_specs=(P("grp", "sep", None, None), P("sep", None, None)),
        check_vma=False,
    )
```

profile of v0, /device:TPU:0, one launch (start us, length us, event | category | flops | bytes accessed | tf_op | source)
XLA Modules:
  0.0 244.2 jit_solution(3018031008141978505)
XLA Ops:
  7.2 0.9 select_reduce_fusion.5
  8.3 0.8 scatter_custom_fusion
  9.2 0.7 all_to_all.9
  9.8 5.2 %all-to-all-start = ((s32[8,1,8]{2,1,0:T(1,128)}), s32[8,1,8]{2,1,0:T(1,128)S(1)}, u32[]{:S(2)}, u32[]{:S(2)}) async-start(s32[8,1,8]{2,1,0:T(1,128)} %bitcast.6), calls=%async_computation | async-start | bytes 8192 | tf_op jit(solution)/shard_map/all_to_all | solution.py:69
  15.3 3.4 %scatter_fusion = bf16[64,64,128]{2,1,0:T(8,128)(2,1)S(1)} fusion(bf16[64,64,128]{2,1,0:T(8,128)(2,1)S(1)} %broadcast_in_dim.90, s32[32]{0:T(128)S(1)} %fusion.44, bf16[32,64,128]{2,1,0:T(8,128)(2,1)} %bitcast.120), kind=kCustom, calls=%fused_computation.2 | custom fusion | bytes 1572992 | tf_op jit(solution)/shard_map/scatter | solution.py:59
  18.7 1.7 copy.28
  20.4 4.2 %all-to-all-start.1 = ((bf16[8,8,64,128]{3,1,2,0:T(8,128)(2,1)}), bf16[8,8,64,128]{3,1,2,0:T(8,128)(2,1)S(1)}, u32[]{:S(2)}, u32[]{:S(2)}) async-start(bf16[8,8,64,128]{3,1,2,0:T(8,128)(2,1)} %copy.28), calls=%async_computation.1 | async-start | bytes 2097152 | tf_op jit(solution)/shard_map/all_to_all | solution.py:62
  24.7 0.6 fusion.45
  26.1 0.5 broadcast.253
  26.6 0.7 reduce.27
  27.4 12.6 %all-to-all-done.1 = bf16[8,8,64,128]{3,1,2,0:T(8,128)(2,1)S(1)} async-done(((bf16[8,8,64,128]{3,1,2,0:T(8,128)(2,1)}), bf16[8,8,64,128]{3,1,2,0:T(8,128)(2,1)S(1)}, u32[]{:S(2)}, u32[]{:S(2)}) %all-to-all-start.1) | async-done | bytes 1048608 | tf_op jit(solution)/shard_map/all_to_all | solution.py:62
  40.0 0.3 fusion.3
  40.3 0.6 copy.30
  40.9 0.7 gather_fusion
  41.7 1.0 copy.31
  42.7 1.6 copy.49
  44.3 2.7 %copy.32 = f32[640,640]{0,1:T(8,128)} copy(f32[640,640]{1,0:T(8,128)} %bitcast.118) | data formatting | bytes 3276800 | tf_op jit(solution)/shard_map/reshape | solution.py:33
  47.0 2.0 fusion.7
  49.0 0.5 select_subtract_fusion
  49.5 1.3 slice.135
  50.8 0.2 copy-done.1
  51.1 1.7 copy.33
  53.0 1.0 copy-done.3
  54.0 11.7 %cholesky.104 = f32[128,128]{1,0:T(8,128)S(1)} custom-call(f32[128,128]{1,0:T(8,128)S(1)} %cholesky.266), custom_call_target="Cholesky" | custom-call | tf_op jit(solution)/shard_map/jit(cholesky)/cholesky | solution.py:36
  65.7 9.8 %custom-call.31 = f32[1,128,128]{1,2,0:T(8,128)S(1)} custom-call(f32[1,128,128]{2,1,0:T(8,128)S(1)} %get-tuple-element.36), custom_call_target="InvertDiagBlocksLowerTriangular" | custom-call | tf_op jit(solution)/shard_map/jit(cholesky)/cholesky | solution.py:36
  75.7 1.2 constant_dynamic-update-slice_fusion.3
  76.9 1.3 convolution_subtract_fusion
  78.2 11.7 %cholesky.217 = f32[128,128]{1,0:T(8,128)S(1)} custom-call(f32[128,128]{1,0:T(8,128)S(1)} %cholesky.270), custom_call_target="Cholesky" | custom-call | tf_op jit(solution)/shard_map/jit(cholesky)/cholesky | solution.py:36
  89.9 9.9 %custom-call.32 = f32[1,128,128]{1,2,0:T(8,128)S(1)} custom-call(f32[1,128,128]{2,1,0:T(8,128)S(1)} %get-tuple-element.33), custom_call_target="InvertDiagBlocksLowerTriangular" | custom-call | tf_op jit(solution)/shard_map/jit(cholesky)/cholesky | solution.py:36
  99.8 0.3 convolution_dynamic-update-slice_fusion
  100.1 1.3 convolution_subtract_fusion.1
  101.4 11.7 %cholesky.238 = f32[128,128]{1,0:T(8,128)S(1)} custom-call(f32[128,128]{1,0:T(8,128)S(1)} %cholesky.275), custom_call_target="Cholesky" | custom-call | tf_op jit(solution)/shard_map/jit(cholesky)/cholesky | solution.py:36
  113.1 0.7 compare_reduce_fusion.1
  113.9 9.8 %custom-call.33 = f32[1,128,128]{1,2,0:T(8,128)S(1)} custom-call(f32[1,128,128]{2,1,0:T(8,128)S(1)} %get-tuple-element.30), custom_call_target="InvertDiagBlocksLowerTriangular" | custom-call | tf_op jit(solution)/shard_map/jit(cholesky)/cholesky | solution.py:36
  123.9 1.2 convolution_subtract_fusion.5
  125.1 11.9 %cholesky.255 = f32[128,128]{1,0:T(8,128)S(1)} custom-call(f32[128,128]{1,0:T(8,128)S(1)} %convolution_subtract_fusion.5), custom_call_target="Cholesky" | custom-call | tf_op jit(solution)/shard_map/jit(cholesky)/cholesky | solution.py:36
  137.1 0.6 compare_reduce_fusion
  137.7 0.6 compare_reduce_fusion.2
  140.9 0.3 fusion.6
  141.2 10.4 %while.1 = (s32[]{:T(128)}, f32[512,512]{1,0:T(8,128)S(1)}, s32[4,2]{0,1:T(2,128)S(1)}, f32[4,128,128]{2,1,0:T(8,128)}, s32[]{:T(128)}) while((s32[]{:T(128)}, f32[512,512]{1,0:T(8,128)S(1)}, s32[4,2]{0,1:T(2,128)S(1)}, f32[4,128,128]{2,1,0:T(8,128)}, s32[]{:T(128)}) %tuple.35), condition=%wide.while_cond, body=%wide.while_body.sunk | while | flops 2 | bytes 132705 | solution.py:37
  141.2 0.5 fusion.58
  141.8 2.0 bitcast_dynamic-update-slice_fusion.2
  143.8 0.5 fusion.58
  144.4 2.0 bitcast_dynamic-update-slice_fusion.2
  146.4 0.5 fusion.58
  147.0 2.0 bitcast_dynamic-update-slice_fusion.2
  149.0 0.5 fusion.58
  149.6 2.0 bitcast_dynamic-update-slice_fusion.2
  151.6 40.1 %custom-call.34 = f32[4,128,128]{1,2,0:T(8,128)S(1)} custom-call(f32[4,128,128]{2,1,0:T(8,128)} %get-tuple-element.9), custom_call_target="InvertDiagBlocksLowerTriangular" | custom-call | tf_op jit(solution)/shard_map/jit(_solve_triangular)/triangular_solve | solution.py:37
  191.7 0.3 fusion.30
  192.2 0.3 fusion.29
  192.5 0.3 convolution_subtract_fusion.2
  192.8 0.3 fusion.27
  193.1 0.3 convolution_subtract_fusion.4
  193.7 0.3 fusion.26
  194.0 0.4 fusion.18
  194.5 2.6 %collective-permute-start.1 = (f32[1,128,128]{2,1,0:T(8,128)S(1)}, f32[1,128,128]{2,1,0:T(8,128)S(1)}, u32[]{:S(2)}, u32[]{:S(2)}) collective-permute-start(f32[1,128,128]{2,1,0:T(8,128)S(1)} %get-tuple-element.26), channel_id=1, source_target_pairs={{0,7},{1,0},{2,1},{3,2},{4,3},{5,4},{6,5},{7,6},{8,15},{9,8},{10,9... | collective-permute-start | bytes 196616 | tf_op jit(solution)/shard_map/ppermute | solution.py:12
  197.1 0.6 collective-permute-start.2
  197.7 2.0 collective-permute-done
  199.7 1.6 collective-permute-done.2
  201.4 0.6 fusion.35
  202.0 1.2 maximum_bitcast_fusion
  203.2 32.7 %all-reduce.3.cloned.1.call-done = f32[1,128,128]{2,1,0:T(8,128)} async-done(((f32[1,128,128]{2,1,0:T(8,128)}), f32[1,128,128]{2,1,0:T(8,128)}) %all-reduce.3.cloned.1.call-update) | async-done | bytes 65552 | tf_op jit(solution)/shard_map/psum | solution.py:86
  235.9 1.5 copy.66
  (55 shorter events, 2.6 us)
Async XLA Ops:
  9.8 10.6 %all-to-all-start = ((s32[8,1,8]{2,1,0:T(1,128)}), s32[8,1,8]{2,1,0:T(1,128)S(1)}, u32[]{:S(2)}, u32[]{:S(2)}) async-start(s32[8,1,8]{2,1,0:T(1,128)} %bitcast.6), calls=%async_computation | async-start | bytes 8192 | tf_op jit(solution)/shard_map/all_to_all | solution.py:69
  18.7 6.0 %copy-start.6 = (s32[1,8]{1,0:T(1,128)S(1)}, s32[1,8]{1,0:T(1,128)}, u32[]{:S(2)}) copy-start(s32[1,8]{1,0:T(1,128)} %param.13) | copy-start | bytes 100
  18.7 6.0 %copy-start.7 = (s32[1,8]{1,0:T(1,128)S(1)}, s32[1,8]{1,0:T(1,128)}, u32[]{:S(2)}) copy-start(s32[1,8]{1,0:T(1,128)} %param.12) | copy-start | bytes 100
  18.7 7.3 %copy-start.8 = (s32[50]{0:T(128)S(1)}, s32[50]{0:T(128)}, u32[]{:S(2)}) copy-start(s32[50]{0:T(128)} %constant.222) | copy-start | bytes 604
  18.7 7.3 %copy-start.4 = (f32[1,8,640]{2,1,0:T(8,128)S(1)}, f32[1,8,640]{2,1,0:T(8,128)}, u32[]{:S(2)}) copy-start(f32[1,8,640]{2,1,0:T(8,128)} %param.14) | copy-start | bytes 61444
  20.4 19.6 %all-to-all-start.1 = ((bf16[8,8,64,128]{3,1,2,0:T(8,128)(2,1)}), bf16[8,8,64,128]{3,1,2,0:T(8,128)(2,1)S(1)}, u32[]{:S(2)}, u32[]{:S(2)}) async-start(bf16[8,8,64,128]{3,1,2,0:T(8,128)(2,1)} %copy.28), calls=%async_computation.1 | async-start | bytes 2097152 | tf_op jit(solution)/shard_map/all_to_all | solution.py:62
  24.6 211.2 %all-reduce.3.cloned.1.call-start = ((), (), s32[]{:S(2)}) async-start(), calls=%async_computation.2 | async-start | bytes 131072 | tf_op jit(solution)/shard_map/psum | solution.py:86
  40.9 0.7 copy-start.5
  47.0 2.0 copy-start
  49.5 1.5 copy-start.1
  51.1 1.7 copy-start.2
  53.0 1.0 copy-start.3
  194.4 5.3 %collective-permute-start = (f32[1,128,128]{2,1,0:T(8,128)S(1)}, f32[1,128,128]{2,1,0:T(8,128)S(1)}, u32[]{:S(2)}, u32[]{:S(2)}) collective-permute-start(f32[1,128,128]{2,1,0:T(8,128)S(1)} %get-tuple-element.24), channel_id=1, source_target_pairs={{0,1},{1,2},{2,3},{3,4},{4,5},{5,6},{6,7},{7,0},{8,9},{9,10},{10,1... | collective-permute-start | bytes 196616 | tf_op jit(solution)/shard_map/ppermute | solution.py:12
  194.5 5.3 %collective-permute-start.1 = (f32[1,128,128]{2,1,0:T(8,128)S(1)}, f32[1,128,128]{2,1,0:T(8,128)S(1)}, u32[]{:S(2)}, u32[]{:S(2)}) collective-permute-start(f32[1,128,128]{2,1,0:T(8,128)S(1)} %get-tuple-element.26), channel_id=1, source_target_pairs={{0,7},{1,0},{2,1},{3,2},{4,3},{5,4},{6,5},{7,6},{8,15},{9,8},{10,9... | collective-permute-start | bytes 196616 | tf_op jit(solution)/shard_map/ppermute | solution.py:12
  197.1 4.3 %collective-permute-start.2 = (f32[1,128,128]{2,1,0:T(8,128)S(1)}, f32[1,128,128]{2,1,0:T(8,128)S(1)}, u32[]{:S(2)}, u32[]{:S(2)}) collective-permute-start(f32[1,128,128]{2,1,0:T(8,128)S(1)} %get-tuple-element.25), channel_id=1, source_target_pairs={{0,4},{1,5},{2,6},{3,7},{4,0},{5,1},{6,2},{7,3},{8,12},{9,13},{10,... | collective-permute-start | bytes 196616 | tf_op jit(solution)/shard_map/ppermute | solution.py:12
Sparse Core Ops, SparseCore 0:
  202.1 33.6 all-reduce.2
where the time goes:
time: 245 us; the launch traced here: 244 us
  other arithmetic  126 us (51%)
  waiting for transfers between devices  49 us (20%)
  local copies, waits for them, and re-layouts  30.5 us (12%)
  between operations  17.7 us (7%)
  starting transfers between devices  12.7 us (5%)
  matrix products  8.06 us (3%)
    another operation x14, other arithmetic, front_factor(): jnp.linalg.cholesky(front_matrix[:elimination_count, :elimination_count])  78.7 us
    another operation x3, other arithmetic, front_factor(): jax.scipy.linalg.solve_triangular(lower_triangle, front_matrix[eliminatio...  40.4 us
    psum x1, waiting for transfers between devices, body(): total = lax.psum(local_sum, 'grp')  32.7 us
    all_to_all x1, waiting for transfers between devices, body(): lax.all_to_all(outgoing.reshape(width, room, rows, column_indices), 'sep'...  12.6 us
    another operation x12, local copies, waits for them, and re-layouts  10.4 us
    another operation x6, matrix products, front_factor(): jnp.linalg.cholesky(front_matrix[:elimination_count, :elimination_count])  5.47 us
    all_to_all x1, starting transfers between devices, body(): lax.all_to_all(labels.reshape(width, room), 'sep', split_axis=0, concat_a...  5.2 us
  transfers between devices with their start and end apart: 6, of which 4 were waited for; matrix products, arithmetic and copies ran while one was open for 3% of the time, Pallas kernels for 0%

commit v1 on v0

--- a/solution.py
+++ b/solution.py
@@ -83,7 +83,7 @@
     for offset in (1, -1, width // 2):
         piece = jnp.where(distance == offset % width, schur, 0.0)[None]
         local_sum = local_sum + passed_along(piece, "sep", offset)
-    total = lax.psum(local_sum, "grp")
+    total = jnp.sum(lax.all_gather(local_sum, axis_name="grp"), 0)
     return (factor[None, None], total)
 
 

time: 245 us -> 211 us (0.86)
  waiting for transfers between devices: 49 us -> 15.2 us
  blocking collectives: 0 us -> 14.7 us
  between operations: 17.7 us -> 4.32 us
    psum x1 -> x0, waiting for transfers between devices: 32.7 us -> none  [body(): total = lax.psum(local_sum, 'grp')]
    all_gather x0 -> x1, blocking collectives: none -> 14.7 us  [body(): total = jnp.sum(lax.all_gather(local_sum, axis_name='grp'), 0)]
  transfers between devices with their start and end apart: 6 -> 5, of which waited for: 4 -> 3; matrix products, arithmetic and copies ran while one was open for 3% -> 4% of each run, Pallas kernels for 0% -> 0%
where the time goes in v1:
time: 211 us; the launch traced here: 210 us
  other arithmetic  126 us (60%)
  local copies, waits for them, and re-layouts  29 us (14%)
  waiting for transfers between devices  15.2 us (7%)
  blocking collectives  14.7 us (7%)
  starting transfers between devices  12.6 us (6%)
  matrix products  8.07 us (4%)
  between operations  4.32 us (2%)
    another operation x14, other arithmetic, front_factor(): jnp.linalg.cholesky(front_matrix[:elimination_count, :elimination_count])  78.7 us
    another operation x3, other arithmetic, front_factor(): jax.scipy.linalg.solve_triangular(lower_triangle, front_matrix[eliminatio...  40.4 us
    all_gather x1, blocking collectives, body(): total = jnp.sum(lax.all_gather(local_sum, axis_name='grp'), 0)  14.7 us
    all_to_all x1, waiting for transfers between devices, body(): lax.all_to_all(outgoing.reshape(width, room, rows, column_indices), 'sep'...  12.7 us
    another operation x12, local copies, waits for them, and re-layouts  10.4 us
    another operation x6, matrix products, front_factor(): jnp.linalg.cholesky(front_matrix[:elimination_count, :elimination_count])  5.47 us
    all_to_all x1, starting transfers between devices, body(): lax.all_to_all(labels.reshape(width, room), 'sep', split_axis=0, concat_a...  5.2 us
  transfers between devices with their start and end apart: 5, of which 3 were waited for; matrix products, arithmetic and copies ran while one was open for 4% of the time, Pallas kernels for 0%

profile of v1, /device:TPU:0, one launch (start us, length us, event | category | flops | bytes accessed | tf_op | source)
XLA Modules:
  0.0 210.2 jit_solution(14879314507736936798)
XLA Ops:
  0.6 0.9 select_reduce_fusion.5
  1.8 0.8 scatter_custom_fusion
  2.6 0.7 all_to_all.9
  3.3 5.2 %all-to-all-start = ((s32[8,1,8]{2,1,0:T(1,128)}), s32[8,1,8]{2,1,0:T(1,128)S(1)}, u32[]{:S(2)}, u32[]{:S(2)}) async-start(s32[8,1,8]{2,1,0:T(1,128)} %bitcast.6), calls=%async_computation | async-start | bytes 8192 | tf_op jit(solution)/shard_map/all_to_all | solution.py:69
  8.5 0.2 broadcast_in_dim.90
  8.7 3.4 %scatter_fusion = bf16[64,64,128]{2,1,0:T(8,128)(2,1)S(1)} fusion(bf16[64,64,128]{2,1,0:T(8,128)(2,1)S(1)} %broadcast_in_dim.90, s32[32]{0:T(128)S(1)} %fusion.44, bf16[32,64,128]{2,1,0:T(8,128)(2,1)} %bitcast.121), kind=kCustom, calls=%fused_computation.2 | custom fusion | bytes 1572992 | tf_op jit(solution)/shard_map/scatter | solution.py:59
  12.2 1.7 copy.28
  13.9 4.2 %all-to-all-start.1 = ((bf16[8,8,64,128]{3,1,2,0:T(8,128)(2,1)}), bf16[8,8,64,128]{3,1,2,0:T(8,128)(2,1)S(1)}, u32[]{:S(2)}, u32[]{:S(2)}) async-start(bf16[8,8,64,128]{3,1,2,0:T(8,128)(2,1)} %copy.28), calls=%async_computation.1 | async-start | bytes 2097152 | tf_op jit(solution)/shard_map/all_to_all | solution.py:62
  18.1 0.6 fusion.45
  19.5 0.5 broadcast.253
  20.0 0.7 reduce.30
  20.8 12.7 %all-to-all-done.1 = bf16[8,8,64,128]{3,1,2,0:T(8,128)(2,1)S(1)} async-done(((bf16[8,8,64,128]{3,1,2,0:T(8,128)(2,1)}), bf16[8,8,64,128]{3,1,2,0:T(8,128)(2,1)S(1)}, u32[]{:S(2)}, u32[]{:S(2)}) %all-to-all-start.1) | async-done | bytes 1048608 | tf_op jit(solution)/shard_map/all_to_all | solution.py:62
  33.4 0.3 fusion.3
  33.7 0.6 copy.30
  34.3 0.7 gather_fusion
  35.2 1.0 copy.31
  36.2 1.6 copy.49
  37.8 2.7 %copy.32 = f32[640,640]{0,1:T(8,128)} copy(f32[640,640]{1,0:T(8,128)} %bitcast.119) | data formatting | bytes 3276800 | tf_op jit(solution)/shard_map/reshape | solution.py:33
  40.5 2.0 fusion.7
  42.5 0.5 select_subtract_fusion
  43.0 1.2 slice.135
  44.2 0.3 copy-done.1
  44.6 1.7 copy.33
  46.5 1.0 copy-done.3
  47.4 11.7 %cholesky.104 = f32[128,128]{1,0:T(8,128)S(1)} custom-call(f32[128,128]{1,0:T(8,128)S(1)} %cholesky.266), custom_call_target="Cholesky" | custom-call | tf_op jit(solution)/shard_map/jit(cholesky)/cholesky | solution.py:36
  59.2 9.8 %custom-call.31 = f32[1,128,128]{1,2,0:T(8,128)S(1)} custom-call(f32[1,128,128]{2,1,0:T(8,128)S(1)} %get-tuple-element.36), custom_call_target="InvertDiagBlocksLowerTriangular" | custom-call | tf_op jit(solution)/shard_map/jit(cholesky)/cholesky | solution.py:36
  69.1 1.2 constant_dynamic-update-slice_fusion.3
  70.4 1.3 convolution_subtract_fusion
  71.6 11.7 %cholesky.217 = f32[128,128]{1,0:T(8,128)S(1)} custom-call(f32[128,128]{1,0:T(8,128)S(1)} %cholesky.270), custom_call_target="Cholesky" | custom-call | tf_op jit(solution)/shard_map/jit(cholesky)/cholesky | solution.py:36
  83.4 9.9 %custom-call.32 = f32[1,128,128]{1,2,0:T(8,128)S(1)} custom-call(f32[1,128,128]{2,1,0:T(8,128)S(1)} %get-tuple-element.33), custom_call_target="InvertDiagBlocksLowerTriangular" | custom-call | tf_op jit(solution)/shard_map/jit(cholesky)/cholesky | solution.py:36
  93.3 0.3 convolution_dynamic-update-slice_fusion
  93.6 1.3 convolution_subtract_fusion.1
  94.9 11.7 %cholesky.238 = f32[128,128]{1,0:T(8,128)S(1)} custom-call(f32[128,128]{1,0:T(8,128)S(1)} %cholesky.275), custom_call_target="Cholesky" | custom-call | tf_op jit(solution)/shard_map/jit(cholesky)/cholesky | solution.py:36
  106.6 0.7 compare_reduce_fusion.1
  107.3 9.8 %custom-call.33 = f32[1,128,128]{1,2,0:T(8,128)S(1)} custom-call(f32[1,128,128]{2,1,0:T(8,128)S(1)} %get-tuple-element.30), custom_call_target="InvertDiagBlocksLowerTriangular" | custom-call | tf_op jit(solution)/shard_map/jit(cholesky)/cholesky | solution.py:36
  117.4 1.2 convolution_subtract_fusion.5
  118.6 11.9 %cholesky.255 = f32[128,128]{1,0:T(8,128)S(1)} custom-call(f32[128,128]{1,0:T(8,128)S(1)} %convolution_subtract_fusion.5), custom_call_target="Cholesky" | custom-call | tf_op jit(solution)/shard_map/jit(cholesky)/cholesky | solution.py:36
  130.5 0.6 compare_reduce_fusion
  131.2 0.6 compare_reduce_fusion.2
  134.4 0.3 fusion.6
  134.6 10.4 %while.1 = (s32[]{:T(128)}, f32[512,512]{1,0:T(8,128)S(1)}, s32[4,2]{0,1:T(2,128)S(1)}, f32[4,128,128]{2,1,0:T(8,128)}, s32[]{:T(128)}) while((s32[]{:T(128)}, f32[512,512]{1,0:T(8,128)S(1)}, s32[4,2]{0,1:T(2,128)S(1)}, f32[4,128,128]{2,1,0:T(8,128)}, s32[]{:T(128)}) %tuple.35), condition=%wide.while_cond, body=%wide.while_body.sunk | while | flops 2 | bytes 132705 | solution.py:37
  134.7 0.5 fusion.58
  135.2 2.0 bitcast_dynamic-update-slice_fusion.2
  137.3 0.5 fusion.58
  137.8 2.0 bitcast_dynamic-update-slice_fusion.2
  139.9 0.5 fusion.58
  140.4 2.0 bitcast_dynamic-update-slice_fusion.2
  142.5 0.5 fusion.58
  143.0 2.0 bitcast_dynamic-update-slice_fusion.2
  145.0 40.1 %custom-call.34 = f32[4,128,128]{1,2,0:T(8,128)S(1)} custom-call(f32[4,128,128]{2,1,0:T(8,128)} %get-tuple-element.9), custom_call_target="InvertDiagBlocksLowerTriangular" | custom-call | tf_op jit(solution)/shard_map/jit(_solve_triangular)/triangular_solve | solution.py:37
  185.2 0.3 fusion.30
  185.7 0.3 fusion.29
  186.0 0.3 convolution_subtract_fusion.2
  186.2 0.3 fusion.27
  186.5 0.3 convolution_subtract_fusion.4
  187.1 0.3 fusion.26
  187.4 0.4 fusion.18
  188.0 2.6 %collective-permute-start.1 = (f32[1,128,128]{2,1,0:T(8,128)S(1)}, f32[1,128,128]{2,1,0:T(8,128)S(1)}, u32[]{:S(2)}, u32[]{:S(2)}) collective-permute-start(f32[1,128,128]{2,1,0:T(8,128)S(1)} %get-tuple-element.26), channel_id=1, source_target_pairs={{0,7},{1,0},{2,1},{3,2},{4,3},{5,4},{6,5},{7,6},{8,15},{9,8},{10,9... | collective-permute-start | bytes 196616 | tf_op jit(solution)/shard_map/ppermute | solution.py:12
  190.6 0.6 collective-permute-start.2
  191.1 1.1 maximum_bitcast_fusion
  192.3 0.9 collective-permute-done
  193.2 1.6 collective-permute-done.2
  194.9 14.7 %all-gather = f32[4,128,128]{2,1,0:T(8,128)S(1)} all-gather(f32[1,128,128]{2,1,0:T(8,128)S(1)} %fusion.35), channel_id=2, replica_groups=mesh['grp'=4,'sep'=8] {'grp'}, dimensions={0}, use_global_device_ids=true | all-gather | bytes 327680 | tf_op jit(solution)/shard_map/all_gather | solution.py:86
  209.6 0.6 reduce.25
  (53 shorter events, 2.3 us)
Async XLA Ops:
  3.3 10.6 %all-to-all-start = ((s32[8,1,8]{2,1,0:T(1,128)}), s32[8,1,8]{2,1,0:T(1,128)S(1)}, u32[]{:S(2)}, u32[]{:S(2)}) async-start(s32[8,1,8]{2,1,0:T(1,128)} %bitcast.6), calls=%async_computation | async-start | bytes 8192 | tf_op jit(solution)/shard_map/all_to_all | solution.py:69
  12.1 6.0 %copy-start.6 = (s32[1,8]{1,0:T(1,128)S(1)}, s32[1,8]{1,0:T(1,128)}, u32[]{:S(2)}) copy-start(s32[1,8]{1,0:T(1,128)} %param.13) | copy-start | bytes 100
  12.1 5.9 %copy-start.7 = (s32[1,8]{1,0:T(1,128)S(1)}, s32[1,8]{1,0:T(1,128)}, u32[]{:S(2)}) copy-start(s32[1,8]{1,0:T(1,128)} %param.12) | copy-start | bytes 100
  12.1 7.3 %copy-start.8 = (s32[50]{0:T(128)S(1)}, s32[50]{0:T(128)}, u32[]{:S(2)}) copy-start(s32[50]{0:T(128)} %constant.222) | copy-start | bytes 604
  12.2 7.3 %copy-start.4 = (f32[1,8,640]{2,1,0:T(8,128)S(1)}, f32[1,8,640]{2,1,0:T(8,128)}, u32[]{:S(2)}) copy-start(f32[1,8,640]{2,1,0:T(8,128)} %param.14) | copy-start | bytes 61444
  13.9 19.6 %all-to-all-start.1 = ((bf16[8,8,64,128]{3,1,2,0:T(8,128)(2,1)}), bf16[8,8,64,128]{3,1,2,0:T(8,128)(2,1)S(1)}, u32[]{:S(2)}, u32[]{:S(2)}) async-start(bf16[8,8,64,128]{3,1,2,0:T(8,128)(2,1)} %copy.28), calls=%async_computation.1 | async-start | bytes 2097152 | tf_op jit(solution)/shard_map/all_to_all | solution.py:62
  34.3 0.7 copy-start.5
  40.5 2.0 copy-start
  43.0 1.5 copy-start.1
  44.5 1.7 copy-start.2
  46.4 1.0 copy-start.3
  187.9 5.3 %collective-permute-start = (f32[1,128,128]{2,1,0:T(8,128)S(1)}, f32[1,128,128]{2,1,0:T(8,128)S(1)}, u32[]{:S(2)}, u32[]{:S(2)}) collective-permute-start(f32[1,128,128]{2,1,0:T(8,128)S(1)} %get-tuple-element.24), channel_id=1, source_target_pairs={{0,1},{1,2},{2,3},{3,4},{4,5},{5,6},{6,7},{7,0},{8,9},{9,10},{10,1... | collective-permute-start | bytes 196616 | tf_op jit(solution)/shard_map/ppermute | solution.py:12
  188.0 5.3 %collective-permute-start.1 = (f32[1,128,128]{2,1,0:T(8,128)S(1)}, f32[1,128,128]{2,1,0:T(8,128)S(1)}, u32[]{:S(2)}, u32[]{:S(2)}) collective-permute-start(f32[1,128,128]{2,1,0:T(8,128)S(1)} %get-tuple-element.26), channel_id=1, source_target_pairs={{0,7},{1,0},{2,1},{3,2},{4,3},{5,4},{6,5},{7,6},{8,15},{9,8},{10,9... | collective-permute-start | bytes 196616 | tf_op jit(solution)/shard_map/ppermute | solution.py:12
  190.6 4.3 %collective-permute-start.2 = (f32[1,128,128]{2,1,0:T(8,128)S(1)}, f32[1,128,128]{2,1,0:T(8,128)S(1)}, u32[]{:S(2)}, u32[]{:S(2)}) collective-permute-start(f32[1,128,128]{2,1,0:T(8,128)S(1)} %get-tuple-element.25), channel_id=1, source_target_pairs={{0,4},{1,5},{2,6},{3,7},{4,0},{5,1},{6,2},{7,3},{8,12},{9,13},{10,... | collective-permute-start | bytes 196616 | tf_op jit(solution)/shard_map/ppermute | solution.py:12
